TPU v7x, 512 devices: a whole 4x8x8 slice. The times are simulated.
512 devices in a mesh: chain: 8 (over x, core), tile: 64 (over y, z).
Axes of the slice: x: 4, y: 8, z: 8, core: 2. Of those that a mesh axis runs over, the one named last changes fastest.
Arguments:
- right_side: float32 [3, 2, 32, 32768], P(None, None, None, ('chain', 'tile')), may hold values from -6 to 6
- diag_inverse: float32 [2, 32768, 4096], P(None, ('chain', 'tile'))
- coupling: float32 [2, 32768, 4096], P(None, ('chain', 'tile')), may hold values from -0.0390625 to 0.0390625
- updates: float32 [131072, 192], P(('chain', 'tile')), may hold values from -2.4 to 2.4
- update_rows: int32 [131072], P(('chain', 'tile')), may hold values from 0 to 4095, as said below
- tile_counts: int32 [1024], P(('chain', 'tile')), may hold values from 32 to 128, as said below
Outputs:
- solution: float32 [3, 2, 32, 32768], P(None, None, None, ('chain', 'tile'))
Inputs may be any that keep to these rules, and one draw needn't show every extreme that they name: `update_rows`: rows are counted within the supernode of the group that holds the entry. In each aligned block of 256 entries (the update rows of one device) at most 8 entries fall in any one aligned range of 64 rows, and in each run of 64 aligned blocks one such range receives exactly 8 entries from every block of the run. Padding rows carry entries too. `tile_counts`: one tile has all 128 rows live.
All inputs are finite; a program needn't handle non-finite values.
Results may differ from a plain program's by a relative error of at most 0.0001.
Values sent between devices are 32-bit elements; how exact they have to be, the bound alone decides.
A program may use at most 64 MiB of HBM per device.

v0:
```python
import jax
import jax.numpy as jnp
from jax import lax
from jax.sharding import PartitionSpec as P

highest = lax.Precision.HIGHEST


def shifted(value, axis, by):
    peers = lax.axis_size(axis)
    pairs = [(i, i + by) for i in range(peers) if 0 <= i + by < peers]
    return lax.ppermute(value, axis, pairs)


def combine_parts(products):
    return jnp.stack([products[0, 0] - products[1, 1], products[0, 1] + products[1, 0]], axis=0)


def body(right_side, diag_inverse, coupling, updates, update_rows, tile_counts):
    batches, halves, sources, own_rows = right_side.shape
    chain_size = lax.axis_size("chain")
    full_rows = diag_inverse.shape[2]
    row_count = updates.shape[0]
    tile_rows = row_count // tile_counts.shape[0]
    limits = jnp.broadcast_to(tile_counts[:, None], (tile_counts.shape[0], tile_rows)).reshape(-1)
    is_live = jnp.arange(row_count, dtype=jnp.int32) % tile_rows < limits
    live_updates = jnp.where(is_live[:, None], updates, 0.0)
    dense_sum = jax.ops.segment_sum(live_updates, update_rows, num_segments=full_rows)
    accumulated = lax.psum_scatter(dense_sum, "tile", scatter_dimension=0, tiled=True)
    arranged = accumulated.reshape(own_rows, batches, halves, sources).transpose(1, 2, 3, 0)
    reduced_all = right_side - arranged
    chain_index = lax.axis_index("chain")
    section_count = chain_size + batches - 1

    def accumulate(columns):
        diag_part = jnp.einsum("jrs,kis->kjri", columns, diag_inverse, precision=highest)
        couple_part = jnp.einsum("jrs,kis->kjri", columns, coupling, precision=highest)
        return (diag_part, couple_part)

    def advance(section_index, loop_state):
        carried, solution = loop_state
        incoming = shifted(carried, "chain", 1)
        batch_index = section_index - chain_index
        active = (batch_index >= 0) & (batch_index < batches)
        clamped = jnp.clip(batch_index, 0, batches - 1)
        reduced = lax.dynamic_index_in_dim(reduced_all, clamped, 0, keepdims=False) - incoming
        diag_sum, couple_sum = accumulate(lax.all_gather(reduced, "tile", axis=2, tiled=True))
        updated = lax.dynamic_update_index_in_dim(solution, combine_parts(diag_sum), clamped, 0)
        return (combine_parts(couple_sum), jnp.where(active, updated, solution))

    start_state = (jnp.zeros((2, sources, own_rows), jnp.float32), jnp.zeros_like(right_side))
    final_carry, solution = lax.fori_loop(0, section_count, advance, start_state)
    return solution


def solution(mesh):
    in_specs = (
        P(None, None, None, ("chain", "tile")),
        P(None, ("chain", "tile"), None),
        P(None, ("chain", "tile"), None),
        P(("chain", "tile"), None),
        P(("chain", "tile")),
        P(("chain", "tile")),
    )
    out_specs = P(None, None, None, ("chain", "tile"))
    return jax.shard_map(body, mesh=mesh, in_specs=in_specs, out_specs=out_specs, check_vma=False)
```

profile of v0, /device:TPU:7, one launch (start us, length us, event | category | flops | bytes accessed | tf_op | source)
XLA Modules:
  0.0 1289.4 jit_solution(14064460779872113943)
XLA Ops:
  8.3 4.2 scatter_custom_fusion
  12.6 247.0 %reduce-scatter.2.cloned.1.call-done = f32[64,192]{1,0:T(8,128)} async-done(((f32[4096,192]{1,0:T(8,128)}), f32[64,192]{1,0:T(8,128)}) %reduce-scatter.2.cloned.1.call-update) | async-done | bytes 49168 | tf_op jit(solution)/shard_map/reduce_scatter | solution.py:29
  260.6 1021.6 %while.15 = (s32[]{:T(128)}, f32[2,32,64]{2,1,0:T(8,128)S(1)}, f32[3,2,32,64]{3,2,1,0:T(8,128)S(1)}, s32[]{:T(128)}, f32[3,2,32,64]{3,2,1,0:T(8,128)S(1)}, /*ind...) while((s32[]{:T(128)}, f32[2,32,64]{2,1,0:T(8,128)S(1)}, ...), condition=%wide.region_3.4_spmd, body=%wide.region_2.3_spmd.sunk | while | flops 805330944 | bytes 23675160 | solution.py:52
  262.2 6.7 collective-permute-done
  269.6 82.7 %all-gather.2.cloned.1.call-done = f32[2,32,4096]{1,0,2:T(2,128)} async-done(((f32[2,32,64]{1,0,2:T(2,128)}), f32[2,32,4096]{1,0,2:T(2,128)}) %all-gather.2.cloned.1.call-update) | async-done | bytes 1048592 | tf_op jit(solution)/shard_map/while/body/eval_jaxpr/all_gather | solution.py:47
  352.3 5.2 copy.48
  360.7 3.1 fusion.41
  365.4 5.8 collective-permute-done
  371.9 82.4 %all-gather.2.cloned.1.call-done = f32[2,32,4096]{1,0,2:T(2,128)} async-done(((f32[2,32,64]{1,0,2:T(2,128)}), f32[2,32,4096]{1,0,2:T(2,128)}) %all-gather.2.cloned.1.call-update) | async-done | bytes 1048592 | tf_op jit(solution)/shard_map/while/body/eval_jaxpr/all_gather | solution.py:47
  454.3 5.2 copy.48
  459.6 3.1 fusion.38
  462.7 3.1 fusion.41
  467.5 5.8 collective-permute-done
  474.0 82.4 %all-gather.2.cloned.1.call-done = f32[2,32,4096]{1,0,2:T(2,128)} async-done(((f32[2,32,64]{1,0,2:T(2,128)}), f32[2,32,4096]{1,0,2:T(2,128)}) %all-gather.2.cloned.1.call-update) | async-done | bytes 1048592 | tf_op jit(solution)/shard_map/while/body/eval_jaxpr/all_gather | solution.py:47
  556.3 5.2 copy.48
  561.6 3.1 fusion.38
  564.8 3.1 fusion.41
  569.5 5.8 collective-permute-done
  576.0 82.4 %all-gather.2.cloned.1.call-done = f32[2,32,4096]{1,0,2:T(2,128)} async-done(((f32[2,32,64]{1,0,2:T(2,128)}), f32[2,32,4096]{1,0,2:T(2,128)}) %all-gather.2.cloned.1.call-update) | async-done | bytes 1048592 | tf_op jit(solution)/shard_map/while/body/eval_jaxpr/all_gather | solution.py:47
  658.4 5.2 copy.48
  663.6 3.1 fusion.38
  666.8 3.1 fusion.41
  671.6 5.8 collective-permute-done
  678.1 82.4 %all-gather.2.cloned.1.call-done = f32[2,32,4096]{1,0,2:T(2,128)} async-done(((f32[2,32,64]{1,0,2:T(2,128)}), f32[2,32,4096]{1,0,2:T(2,128)}) %all-gather.2.cloned.1.call-update) | async-done | bytes 1048592 | tf_op jit(solution)/shard_map/while/body/eval_jaxpr/all_gather | solution.py:47
  760.4 5.2 copy.48
  768.8 3.1 fusion.41
  773.6 5.8 collective-permute-done
  780.1 82.4 %all-gather.2.cloned.1.call-done = f32[2,32,4096]{1,0,2:T(2,128)} async-done(((f32[2,32,64]{1,0,2:T(2,128)}), f32[2,32,4096]{1,0,2:T(2,128)}) %all-gather.2.cloned.1.call-update) | async-done | bytes 1048592 | tf_op jit(solution)/shard_map/while/body/eval_jaxpr/all_gather | solution.py:47
  862.5 5.2 copy.48
  867.7 3.1 fusion.38
  870.9 3.1 fusion.41
  875.6 5.8 collective-permute-done
  882.1 82.4 %all-gather.2.cloned.1.call-done = f32[2,32,4096]{1,0,2:T(2,128)} async-done(((f32[2,32,64]{1,0,2:T(2,128)}), f32[2,32,4096]{1,0,2:T(2,128)}) %all-gather.2.cloned.1.call-update) | async-done | bytes 1048592 | tf_op jit(solution)/shard_map/while/body/eval_jaxpr/all_gather | solution.py:47
  964.5 5.2 copy.48
  969.7 3.1 fusion.38
  972.9 3.1 fusion.41
  977.7 5.8 collective-permute-done
  984.2 82.4 %all-gather.2.cloned.1.call-done = f32[2,32,4096]{1,0,2:T(2,128)} async-done(((f32[2,32,64]{1,0,2:T(2,128)}), f32[2,32,4096]{1,0,2:T(2,128)}) %all-gather.2.cloned.1.call-update) | async-done | bytes 1048592 | tf_op jit(solution)/shard_map/while/body/eval_jaxpr/all_gather | solution.py:47
  1066.5 5.2 copy.48
  1074.9 3.1 fusion.41
  1079.7 5.8 collective-permute-done
  1086.2 82.4 %all-gather.2.cloned.1.call-done = f32[2,32,4096]{1,0,2:T(2,128)} async-done(((f32[2,32,64]{1,0,2:T(2,128)}), f32[2,32,4096]{1,0,2:T(2,128)}) %all-gather.2.cloned.1.call-update) | async-done | bytes 1048592 | tf_op jit(solution)/shard_map/while/body/eval_jaxpr/all_gather | solution.py:47
  1168.6 5.2 copy.48
  1177.0 3.1 fusion.41
  1181.8 5.8 collective-permute-done
  1188.2 82.4 %all-gather.2.cloned.1.call-done = f32[2,32,4096]{1,0,2:T(2,128)} async-done(((f32[2,32,64]{1,0,2:T(2,128)}), f32[2,32,4096]{1,0,2:T(2,128)}) %all-gather.2.cloned.1.call-update) | async-done | bytes 1048592 | tf_op jit(solution)/shard_map/while/body/eval_jaxpr/all_gather | solution.py:47
  1270.6 5.2 copy.48
  1279.0 3.1 fusion.41
  (170 shorter events, 41.6 us)
Async XLA Ops:
  6.5 253.0 %reduce-scatter.2.cloned.1.call-start = ((), (), s32[]{:S(2)}) async-start(), calls=%async_computation.1 | async-start | bytes 4259840 | tf_op jit(solution)/shard_map/reduce_scatter | solution.py:29
  12.6 247.9 %copy-start.3 = (f32[3,2,32,64]{3,2,1,0:T(8,128)S(1)}, f32[3,2,32,64]{3,2,1,0:T(8,128)}, u32[]{:S(2)}) copy-start(f32[3,2,32,64]{3,2,1,0:T(8,128)} %param.8) | copy-start | bytes 147460
  12.6 248.0 %copy-start = (f32[2,64,4096]{2,1,0:T(8,128)S(1)}, f32[2,64,4096]{2,1,0:T(8,128)}, u32[]{:S(2)}) copy-start(f32[2,64,4096]{2,1,0:T(8,128)} %param.10) | copy-start | bytes 6291460
  260.6 91.7 %all-gather.2.cloned.1.call-start = ((), (), s32[]{:S(2)}) async-start(), calls=%async_computation.2 | async-start | bytes 4259840 | tf_op jit(solution)/shard_map/while/body/eval_jaxpr/all_gather | solution.py:47
  260.7 8.1 collective-permute-start
  357.5 3.2 copy-start.1
  363.9 90.4 %all-gather.2.cloned.1.call-start = ((), (), s32[]{:S(2)}) async-start(), calls=%async_computation.2 | async-start | bytes 4259840 | tf_op jit(solution)/shard_map/while/body/eval_jaxpr/all_gather | solution.py:47
  364.0 7.2 collective-permute-start
  459.5 3.2 copy-start.1
  465.9 90.4 %all-gather.2.cloned.1.call-start = ((), (), s32[]{:S(2)}) async-start(), calls=%async_computation.2 | async-start | bytes 4259840 | tf_op jit(solution)/shard_map/while/body/eval_jaxpr/all_gather | solution.py:47
  466.1 7.2 collective-permute-start
  561.6 3.2 copy-start.1
  568.0 90.4 %all-gather.2.cloned.1.call-start = ((), (), s32[]{:S(2)}) async-start(), calls=%async_computation.2 | async-start | bytes 4259840 | tf_op jit(solution)/shard_map/while/body/eval_jaxpr/all_gather | solution.py:47
  568.1 7.2 collective-permute-start
  663.6 3.2 copy-start.1
  670.0 90.4 %all-gather.2.cloned.1.call-start = ((), (), s32[]{:S(2)}) async-start(), calls=%async_computation.2 | async-start | bytes 4259840 | tf_op jit(solution)/shard_map/while/body/eval_jaxpr/all_gather | solution.py:47
  670.1 7.2 collective-permute-start
  765.7 3.2 copy-start.1
  772.0 90.4 %all-gather.2.cloned.1.call-start = ((), (), s32[]{:S(2)}) async-start(), calls=%async_computation.2 | async-start | bytes 4259840 | tf_op jit(solution)/shard_map/while/body/eval_jaxpr/all_gather | solution.py:47
  772.2 7.2 collective-permute-start
  867.7 3.2 copy-start.1
  874.1 90.4 %all-gather.2.cloned.1.call-start = ((), (), s32[]{:S(2)}) async-start(), calls=%async_computation.2 | async-start | bytes 4259840 | tf_op jit(solution)/shard_map/while/body/eval_jaxpr/all_gather | solution.py:47
  874.2 7.2 collective-permute-start
  969.7 3.2 copy-start.1
  976.1 90.4 %all-gather.2.cloned.1.call-start = ((), (), s32[]{:S(2)}) async-start(), calls=%async_computation.2 | async-start | bytes 4259840 | tf_op jit(solution)/shard_map/while/body/eval_jaxpr/all_gather | solution.py:47
  976.3 7.2 collective-permute-start
  1071.8 3.2 copy-start.1
  1078.2 90.4 %all-gather.2.cloned.1.call-start = ((), (), s32[]{:S(2)}) async-start(), calls=%async_computation.2 | async-start | bytes 4259840 | tf_op jit(solution)/shard_map/while/body/eval_jaxpr/all_gather | solution.py:47
  1078.3 7.2 collective-permute-start
  1173.8 3.2 copy-start.1
  1180.2 90.4 %all-gather.2.cloned.1.call-start = ((), (), s32[]{:S(2)}) async-start(), calls=%async_computation.2 | async-start | bytes 4259840 | tf_op jit(solution)/shard_map/while/body/eval_jaxpr/all_gather | solution.py:47
  1180.3 7.2 collective-permute-start
  1275.8 3.2 copy-start.1
  1282.2 0.6 copy-start.2
Sparse Core Ops, SparseCore 0:
  12.7 246.7 reduce-scatter.1
  269.7 82.5 all-gather.1
  372.0 82.2 all-gather.1
  474.1 82.2 all-gather.1
  576.1 82.2 all-gather.1
  678.2 82.2 all-gather.1
  780.2 82.2 all-gather.1
  882.2 82.2 all-gather.1
  984.3 82.2 all-gather.1
  1086.3 82.2 all-gather.1
  1188.4 82.2 all-gather.1
where the time goes:
time: 1290 us
  waiting for transfers between devices  1130 us (88%)
  matrix products  62.6 us (5%)
  local copies, waits for them, and re-layouts  56.1 us (4%)
  starting transfers between devices  13.3 us (1%)
  between operations  13.1 us (1%)
  other arithmetic  13 us (1%)
    all_gather x10, waiting for transfers between devices, advance(): lax.all_gather(reduced, 'tile', axis=2, tiled=True)  824 us
    reduce_scatter x1, waiting for transfers between devices, body(): lax.psum_scatter(dense_sum, 'tile', scatter_dimension=0, tiled=True)  247 us
    ppermute x10, waiting for transfers between devices, shifted(): return lax.ppermute(value, axis, pairs)  58.8 us
    all_gather x10, local copies, waits for them, and re-layouts, advance(): lax.all_gather(reduced, 'tile', axis=2, tiled=True)  52.3 us
    dot_general x10, matrix products, accumulate(): jnp.einsum('jrs,kis->kjri', columns, diag_inverse, precision=highest)  31.3 us
    dot_general x10, matrix products, accumulate(): jnp.einsum('jrs,kis->kjri', columns, coupling, precision=highest)  31.2 us
  transfers between devices with their start and end apart: 21, of which 21 were waited for; matrix products, arithmetic and copies ran while one was open for 0% of the time, Pallas kernels for 0%

commit v1 on v0

v1 whole, which is shorter than its diff:
```python
import functools

import jax
import jax.numpy as jnp
from jax import lax
from jax.experimental import pallas as pl
from jax.experimental.pallas import tpu as pltpu
from jax.sharding import PartitionSpec as P

MESH = pl.DeviceIdType.MESH
F32 = jnp.float32
BF16 = jnp.bfloat16
SIDE = 8
SLOTS = 8
LANES = 128


def remote(src, dst, send_sem, recv_sem, device):
    return pltpu.make_async_remote_copy(
        src_ref=src, dst_ref=dst, send_sem=send_sem, recv_sem=recv_sem, device_id=device, device_id_type=MESH
    )


def split(value):
    high = value.astype(BF16)
    return high, (value - high.astype(F32)).astype(BF16)


def iota(shape, axis):
    return lax.broadcasted_iota(jnp.int32, shape, axis)


def kernel(chains, rhs, upd, rows, counts, diag, coup, out, wide, slots_out, slots_in, first, second,
           first_hi, first_lo, second_hi, second_lo, base, zbuf, part_in, part_out, diag_in, diag_out, stack,
           local_sem, slot_send, slot_recv, mat_send, mat_recv, z_send, z_recv, y_send, y_recv, d_send, d_recv):
    pieces, fold_rows = rhs.shape[0], rhs.shape[1]
    own = 2 * fold_rows
    group = SIDE * SIDE
    span = SIDE * own
    chain = lax.axis_index("chain")
    me = lax.axis_index("tile")
    y, z = me // SIDE, me % SIDE
    not_last = chain < chains - 1
    last = chain == chains - 1

    barrier = pltpu.get_barrier_semaphore()

    def greet(offset, carry):
        pl.semaphore_signal(barrier, inc=1, device_id=(chain, (me + offset) % group), device_id_type=MESH)
        return carry

    lax.fori_loop(1, group, greet, 0)

    @pl.when(not_last)
    def _():
        for row in range(SIDE):
            pl.semaphore_signal(barrier, inc=1, device_id=(chain + 1, row * SIDE + z), device_id_type=MESH)

    @pl.when(chain > 0)
    def _():
        for row in range(SIDE):
            pl.semaphore_signal(barrier, inc=1, device_id=(chain - 1, row * SIDE + z), device_id_type=MESH)

    count_rows = upd.shape[0]
    columns = upd.shape[1]
    wide[...] = jnp.zeros_like(wide)
    wide[:, :columns] = upd[...]
    row_of = rows[...]
    owner = lax.div(row_of, own)
    local = (row_of - owner * own).astype(F32)
    lane = iota((1, count_rows), 1)
    half = count_rows // 2
    live = jnp.where(lane < half, lane, lane - half) < jnp.where(lane < half, counts[0], counts[1])
    hits = (iota((group, count_rows), 0) == owner).astype(F32)
    before = (iota((count_rows, count_rows), 0) < iota((count_rows, count_rows), 1)).astype(F32).astype(BF16)
    earlier = jnp.dot(hits.astype(BF16), before, preferred_element_type=F32)
    rank = jnp.sum(hits * earlier, axis=0, keepdims=True)
    slot = jnp.where(live, owner.astype(F32) * SLOTS + rank, -1.0)
    pick = iota((group * SLOTS, count_rows), 0).astype(F32) == slot
    place = jnp.sum(jnp.where(pick, local, 0.0), axis=1, keepdims=True)
    pick = pick.astype(F32).astype(BF16)
    high, low = split(wide[...])
    payload = jnp.dot(pick, high, preferred_element_type=F32) + jnp.dot(pick, low, preferred_element_type=F32)
    payload = jnp.where(iota(payload.shape, 1) == columns, place, payload)
    slots_out[...] = payload.reshape(slots_out.shape)

    ends = (chain == 0) | last

    @pl.when(ends)
    def _():
        pl.semaphore_wait(barrier, group - 1 + SIDE)

    @pl.when(jnp.logical_not(ends))
    def _():
        pl.semaphore_wait(barrier, group - 1 + 2 * SIDE)

    def send_slots(offset, carry):
        peer = (me + offset) % group
        remote(slots_out.at[peer], slots_in.at[me], slot_send, slot_recv, (chain, peer)).start()
        return carry

    lax.fori_loop(1, group, send_slots, 0)
    slots_in[me] = slots_out[me]

    def columns_of(source, row):
        return source.at[:, :, pl.ds(pl.multiple_of(row * span, span), span)]

    def send_matrix(source, target, which):
        pltpu.make_async_copy(columns_of(source, y), target.at[y], local_sem.at[which]).start()
        for offset in (4, 3, 5, 2, 6, 1, 7):
            row = (y + offset) % SIDE
            remote(columns_of(source, row), target.at[y], mat_send.at[which], mat_recv.at[which],
                   (chain, row * SIDE + z)).start()

    def take_matrix(source, target, which, hi, lo):
        pltpu.make_async_copy(columns_of(source, y), target.at[y], local_sem.at[which]).wait()
        seven = target.at[pl.ds(0, SIDE - 1)]
        remote(seven, seven, mat_send.at[which], mat_recv.at[which], (chain, me)).wait_recv()

        def cut(row, carry):
            for part in range(2):
                high, low = split(target[row, part])
                at = pl.ds(pl.multiple_of(row * own, own), own)
                hi[at, part * span:(part + 1) * span] = high
                lo[at, part * span:(part + 1) * span] = low
            return carry

        lax.fori_loop(0, SIDE, cut, 0)

    @pl.when(not_last)
    def _():
        send_matrix(coup, first, 0)

    @pl.when(last)
    def _():
        send_matrix(diag, first, 0)

    most = slots_in.at[pl.ds(0, group - 1)]
    remote(most, most, slot_send, slot_recv, (chain, me)).wait_recv()
    arrived = slots_in[...].reshape(group * SLOTS, slots_in.shape[2])
    pick = (arrived[:, columns:columns + 1] == iota((group * SLOTS, own), 1).astype(F32)).astype(F32).astype(BF16)
    high, low = split(arrived)
    across = (((0,), (0,)), ((), ()))
    total = (lax.dot_general(pick, high, across, preferred_element_type=F32)
             + lax.dot_general(pick, low, across, preferred_element_type=F32))
    left = iota((fold_rows, LANES), 1) < LANES // 2
    for piece in range(pieces):
        tile = total[:, (piece // 2) * LANES:(piece // 2 + 1) * LANES]
        top, bottom = tile[:fold_rows], tile[fold_rows:]
        if piece % 2 == 0:
            folded = jnp.where(left, top, pltpu.roll(bottom, LANES // 2, 1))
        else:
            folded = jnp.where(left, pltpu.roll(top, LANES // 2, 1), bottom)
        base[piece] = rhs[piece] - folded

    take_matrix(coup, first, 0, first_hi, first_lo)

    @pl.when(not_last)
    def _():
        send_matrix(diag, second, 1)

    def begin(piece):
        @pl.when(chain == 0)
        def _():
            zbuf[piece, z] = base[piece]

        @pl.when(chain > 0)
        def _():
            remote(part_in.at[piece], part_in.at[piece], y_send.at[piece], y_recv.at[piece], (chain, me)).wait_recv()
            zbuf[piece, z] = base[piece] - jnp.sum(part_in[piece], axis=0)

        for offset in (4, 3, 5, 2, 6, 1, 7):
            peer = (z + offset) % SIDE
            remote(zbuf.at[piece, z], zbuf.at[piece, z], z_send.at[piece], z_recv.at[piece],
                   (chain, y * SIDE + peer)).start()

    def multiply(piece, hi, lo, target):
        both = stack[piece]
        wide_sum = jnp.dot(hi[...], both, preferred_element_type=F32)
        narrow = jnp.dot(lo[...], both[:, :LANES], preferred_element_type=F32)
        sums = wide_sum[:, :LANES] + wide_sum[:, LANES:] + narrow
        for row in range(SIDE):
            top = sums[row * own:row * own + fold_rows]
            bottom = sums[row * own + fold_rows:(row + 1) * own]
            target[piece, row] = jnp.where(left, top, bottom)

    def send_diag(piece):
        diag_in[piece, y] = diag_out[piece, y]
        for offset in (4, 3, 5, 2, 6, 1, 7):
            row = (y + offset) % SIDE
            remote(diag_out.at[piece, row], diag_in.at[piece, y], d_send.at[piece], d_recv.at[piece],
                   (chain, row * SIDE + z)).start()

    def finish(piece):
        seven = zbuf.at[piece, pl.ds(0, SIDE - 1)]
        remote(seven, seven, z_send.at[piece], z_recv.at[piece], (chain, me)).wait_recv()
        lane = iota((fold_rows, LANES), 1)
        imag = lane % (LANES // 2) >= LANES // 4
        for source in range(SIDE):
            block = zbuf[piece, source]
            turned = jnp.where(imag, pltpu.roll(block, LANES // 4, 1), -pltpu.roll(block, LANES - LANES // 4, 1))
            for part, value in enumerate((block, turned)):
                other = pltpu.roll(value, LANES // 2, 1)
                for side, wanted in enumerate((jnp.where(left, value, other), jnp.where(left, other, value))):
                    high, low = split(wanted)
                    at = part * span + source * own + side * fold_rows
                    stack[piece, at:at + fold_rows, :LANES] = high
                    stack[piece, at:at + fold_rows, LANES:] = low

        @pl.when(not_last)
        def _():
            multiply(piece, first_hi, first_lo, part_out)
            for row in range(SIDE):
                remote(part_out.at[piece, row], part_in.at[piece, y], y_send.at[piece], y_recv.at[piece],
                       (chain + 1, row * SIDE + z)).start()

        @pl.when(last)
        def _():
            multiply(piece, first_hi, first_lo, diag_out)
            send_diag(piece)

    def step(index, carry):
        @pl.when(index < pieces)
        def _():
            begin(index)

        @pl.when(index > 0)
        def _():
            finish(index - 1)

        return carry

    lax.fori_loop(0, pieces + 1, step, 0)

    @pl.when(not_last)
    def _():
        take_matrix(diag, second, 1, second_hi, second_lo)

        def solve(piece, carry):
            multiply(piece, second_hi, second_lo, diag_out)
            send_diag(piece)
            return carry

        lax.fori_loop(0, pieces, solve, 0)

    def collect(piece, carry):
        seven = diag_in.at[piece, pl.ds(0, SIDE - 1)]
        remote(seven, seven, d_send.at[piece], d_recv.at[piece], (chain, me)).wait_recv()
        out[piece] = jnp.sum(diag_in[piece], axis=0)
        return carry

    lax.fori_loop(0, pieces, collect, 0)

    remote(most, most, slot_send, slot_recv, (chain, me)).wait_send()
    seven = first.at[pl.ds(0, SIDE - 1)]
    remote(seven, seven, mat_send.at[0], mat_recv.at[0], (chain, me)).wait_send()

    @pl.when(not_last)
    def _():
        seven = second.at[pl.ds(0, SIDE - 1)]
        remote(seven, seven, mat_send.at[1], mat_recv.at[1], (chain, me)).wait_send()

    def drain(piece, carry):
        seven = zbuf.at[piece, pl.ds(0, SIDE - 1)]
        remote(seven, seven, z_send.at[piece], z_recv.at[piece], (chain, me)).wait_send()
        seven = diag_out.at[piece, pl.ds(0, SIDE - 1)]
        remote(seven, seven, d_send.at[piece], d_recv.at[piece], (chain, me)).wait_send()

        @pl.when(not_last)
        def _():
            remote(part_out.at[piece], part_out.at[piece], y_send.at[piece], y_recv.at[piece], (chain, me)).wait_send()

        return carry

    lax.fori_loop(0, pieces, drain, 0)


def body(chains, right_side, diag_inverse, coupling, updates, update_rows, tile_counts):
    pieces, halves, sources, own = right_side.shape
    fold_rows = own // 2
    group = SIDE * SIDE
    span = SIDE * own
    count_rows = updates.shape[0]
    folded = right_side.reshape(pieces, halves, sources, 2, fold_rows).transpose(0, 4, 3, 1, 2)
    folded = folded.reshape(pieces, fold_rows, LANES)
    vmem = pl.BlockSpec(memory_space=pltpu.VMEM)
    hbm = pl.BlockSpec(memory_space=pl.ANY)
    block = (pieces, SIDE, fold_rows, LANES)
    dma = pltpu.SemaphoreType.DMA
    solved = pl.pallas_call(
        functools.partial(kernel, chains),
        out_shape=jax.ShapeDtypeStruct(folded.shape, F32),
        in_specs=[vmem, vmem, vmem, pl.BlockSpec(memory_space=pltpu.SMEM), hbm, hbm],
        out_specs=vmem,
        scratch_shapes=[
            pltpu.VMEM((count_rows, 2 * LANES), F32),
            pltpu.VMEM((group, SLOTS, 2 * LANES), F32),
            pltpu.VMEM((group, SLOTS, 2 * LANES), F32),
            pltpu.VMEM((SIDE, 2, own, span), F32),
            pltpu.VMEM((SIDE, 2, own, span), F32),
            pltpu.VMEM((span, 2 * span), BF16),
            pltpu.VMEM((span, 2 * span), BF16),
            pltpu.VMEM((span, 2 * span), BF16),
            pltpu.VMEM((span, 2 * span), BF16),
            pltpu.VMEM((pieces, fold_rows, LANES), F32),
            pltpu.VMEM(block, F32),
            pltpu.VMEM(block, F32),
            pltpu.VMEM(block, F32),
            pltpu.VMEM(block, F32),
            pltpu.VMEM(block, F32),
            pltpu.VMEM((pieces, 2 * span, 2 * LANES), BF16),
            dma((2,)),
            dma,
            dma,
            dma((2,)),
            dma((2,)),
            dma((pieces,)),
            dma((pieces,)),
            dma((pieces,)),
            dma((pieces,)),
            dma((pieces,)),
            dma((pieces,)),
        ],
        compiler_params=pltpu.CompilerParams(collective_id=0, has_side_effects=True, vmem_limit_bytes=48 << 20),
    )(folded, updates, update_rows.reshape(1, count_rows), tile_counts, diag_inverse, coupling)
    solved = solved.reshape(pieces, fold_rows, 2, halves, sources).transpose(0, 3, 4, 2, 1)
    return solved.reshape(right_side.shape)


def solution(mesh):
    in_specs = (
        P(None, None, None, ("chain", "tile")),
        P(None, ("chain", "tile"), None),
        P(None, ("chain", "tile"), None),
        P(("chain", "tile"), None),
        P(("chain", "tile")),
        P(("chain", "tile")),
    )
    out_specs = P(None, None, None, ("chain", "tile"))
    run = functools.partial(body, mesh.shape["chain"])
    return jax.shard_map(run, mesh=mesh, in_specs=in_specs, out_specs=out_specs, check_vma=False)
```

time: 1290 us -> 217 us (0.17)
  waiting for transfers between devices: 1130 us -> 0 us
  Pallas kernels: 0 us -> 208 us
  matrix products: 62.6 us -> 0 us
  local copies, waits for them, and re-layouts: 56.1 us -> 8.11 us
  starting transfers between devices: 13.3 us -> 0 us
  between operations: 13.1 us -> 0.06 us
  other arithmetic: 13 us -> 0 us
    all_gather x10 -> x0, waiting for transfers between devices: 824 us -> none  [advance(): lax.all_gather(reduced, 'tile', axis=2, tiled=True)]
    reduce_scatter x1 -> x0, waiting for transfers between devices: 247 us -> none  [body(): lax.psum_scatter(dense_sum, 'tile', scatter_dimension=0, tiled=True)]
    pallas_call x0 -> x1, Pallas kernels: none -> 208 us  [body(): pl.pallas_call(functools.partial(kernel, chains), out_shape=jax.ShapeDtyp...]
    dot_general x20 -> x0, matrix products: 62.6 us -> none  [the longest x10 31.3 us: accumulate(): jnp.einsum('jrs,kis->kjri', columns, diag_inverse, precision=highest)]
    ppermute x10 -> x0, waiting for transfers between devices: 58.8 us -> none  [shifted(): return lax.ppermute(value, axis, pairs)]
    all_gather x10 -> x0, local copies, waits for them, and re-layouts: 52.3 us -> none  [advance(): lax.all_gather(reduced, 'tile', axis=2, tiled=True)]
    ppermute x10 -> x0, starting transfers between devices: 12.9 us -> none  [shifted(): return lax.ppermute(value, axis, pairs)]
  transfers between devices with their start and end apart: 21 -> 0, of which waited for: 21 -> 0; matrix products, arithmetic and copies ran while one was open for 0% -> 0% of each run, Pallas kernels for 0% -> 0%
where the time goes in v1:
time: 217 us; the launch traced here: 216 us
  Pallas kernels  208 us (96%)
  local copies, waits for them, and re-layouts  8.11 us (4%)
    pallas_call x1, Pallas kernels, body(): pl.pallas_call(functools.partial(kernel, chains), out_shape=jax.ShapeDtyp...  208 us
    unnamed x9, local copies, waits for them, and re-layouts  5.57 us

profile of v1, /device:TPU:7, one launch (start us, length us, event | category | flops | bytes accessed | tf_op | source)
XLA Modules:
  0.0 216.4 jit_solution(5351698417700749844)
XLA Ops:
  0.0 1.0 reshape.15
  1.1 0.2 copy.7
  1.2 0.2 reshape.16.rhs
  1.4 1.1 copy.8.upd
  2.5 0.0 copy-start
  2.5 1.6 copy-done
  4.1 0.0 copy-start.1
  4.1 1.6 copy-done.1
  5.7 0.0 copy-start.2
  5.7 0.7 copy-done.2
  6.3 0.0 copy-start.3
  6.4 0.7 copy-done.3
  7.0 208.3 %shard_map.64 = f32[3,32,128]{2,1,0:T(8,128)S(1)} custom-call(f32[3,32,128]{2,1,0:T(8,128)S(1)} %reshape.16.rhs, f32[256,192]{1,0:T(8,128)S(1)} %copy.8.upd, s32[1,256]{1,0:T(1,128)S(1)} %bitcast.5, s32[2]{0:T(128)S(1)} %copy-done.3, f32[2,64,4096]{2,1,0:T(8,128)S(1)} %copy-done, f32[2,64,4096]{2,1,0:T(8,128)S(1)} %copy-done.1), custom_call_target="tpu_custom_call" | custom-call | tf_op jit(solution)/shard_map/pallas_call | solution.py:290
  215.3 0.2 reshape.18
  215.5 0.1 copy.9
  215.6 0.8 reshape.19
Async XLA Ops:
  2.5 1.6 copy-start
  4.1 1.6 copy-start.1
  5.7 0.7 copy-start.2
  6.3 0.7 copy-start.3

commit v2 on v1

v2 whole, which is shorter than its diff:
```python
import functools

import jax
import jax.numpy as jnp
from jax import lax
from jax.experimental import pallas as pl
from jax.experimental.pallas import tpu as pltpu
from jax.sharding import PartitionSpec as P

MESH = pl.DeviceIdType.MESH
F32 = jnp.float32
BF16 = jnp.bfloat16
SIDE = 8
FOLD = 4
SLOTS = 8
LANES = 128


def remote(src, dst, send_sem, recv_sem, device):
    return pltpu.make_async_remote_copy(
        src_ref=src, dst_ref=dst, send_sem=send_sem, recv_sem=recv_sem, device_id=device, device_id_type=MESH
    )


def split(value):
    high = value.astype(BF16)
    return high, (value - high.astype(F32)).astype(BF16)


def iota(shape, axis):
    return lax.broadcasted_iota(jnp.int32, shape, axis)


def kernel(chains, rhs, upd, rows, counts, diag, coup, out, wide, slots_out, slots_in, raw, sorted_first, sorted_second, first, second,
           first_hi, first_lo, second_hi, second_lo, rhs_wide, base, zbuf, part_in, part_out, diag_in, diag_out, stack,
           local_sem, slot_send, slot_recv, mat_send, mat_recv, z_send, z_recv, y_send, y_recv, d_send, d_recv, core_done):
    pieces, fold_rows = base.shape[0], base.shape[1]
    own = rhs.shape[1]
    fold = own // fold_rows
    width = LANES // fold
    lane_group = lax.div(iota((fold_rows, LANES), 1), width)
    group = SIDE * SIDE
    span = SIDE * own
    chain = lax.axis_index("chain")
    me = lax.axis_index("tile")
    y, z = me // SIDE, me % SIDE
    not_last = chain < chains - 1
    last = chain == chains - 1
    odd = chain % 2
    across, along = y * odd + z * (1 - odd), z * odd + y * (1 - odd)
    across_step, along_step = 1 + (SIDE - 1) * odd, SIDE - (SIDE - 1) * odd

    def place_of(across_at, along_at):
        return across_at * across_step + along_at * along_step

    def folded(parts):
        result = parts[fold - 1]
        for index in range(fold - 1):
            result = jnp.where(lane_group == index, parts[index], result)
        return result

    def spread(value):
        turns = [value] + [pltpu.roll(value, index * width, 1) for index in range(1, fold)]
        result = []
        for index in range(fold):
            wanted = turns[(fold - 1 - index) % fold]
            for at in range(fold - 1):
                wanted = jnp.where(lane_group == at, turns[(at - index) % fold], wanted)
            result.append(wanted)
        return result

    barrier = pltpu.get_barrier_semaphore()

    def greet(offset, carry):
        pl.semaphore_signal(barrier, inc=1, device_id=(chain, (me + offset) % group), device_id_type=MESH)
        return carry

    lax.fori_loop(1, group, greet, 0)

    @pl.when(not_last)
    def _():
        for row in range(SIDE):
            pl.semaphore_signal(barrier, inc=1, device_id=(chain + 1, place_of(across, row)), device_id_type=MESH)

    @pl.when(chain > 0)
    def _():
        for row in range(SIDE):
            pl.semaphore_signal(barrier, inc=1, device_id=(chain - 1, place_of(row, along)), device_id_type=MESH)

    def load(source, which):
        pltpu.make_async_copy(source, raw, local_sem.at[which]).start()

    def order(ordered, which):
        pltpu.make_async_copy(raw, raw, local_sem.at[which]).wait()
        near = iota((own, LANES), 1) < LANES // 2

        def pair(index, carry):
            for part in range(2):
                for group_at in range(SIDE // 2):
                    begin_at = [pl.multiple_of((2 * group_at + k) * span + index * LANES, LANES) for k in range(2)]
                    one, two = [raw[part, :, pl.ds(at, LANES)] for at in begin_at]
                    lanes = slice(group_at * LANES, (group_at + 1) * LANES)
                    ordered[2 * index, part, :, lanes] = jnp.where(near, one, pltpu.roll(two, LANES // 2, 1))
                    ordered[2 * index + 1, part, :, lanes] = jnp.where(near, pltpu.roll(one, LANES // 2, 1), two)
            return carry

        lax.fori_loop(0, SIDE // 2, pair, 0)

    @pl.when((odd == 1) & not_last)
    def _():
        load(coup, 0)

    @pl.when(last)
    def _():
        load(diag, 0)

    columns, count_rows = upd.shape
    some = width // 2
    wide[columns:] = jnp.zeros_like(wide[columns:])
    rhs_wide[columns:] = jnp.zeros_like(rhs_wide[columns:])
    per_batch = LANES // (2 * width)
    for piece in range(pieces):
        for part in range(2):
            source = (piece // per_batch) * (LANES // 2) + part * (LANES // 4) + (piece % per_batch) * some
            target = piece * width + part * some
            wide[target:target + some] = upd[source:source + some]
            rhs_wide[target:target + some] = rhs[source:source + some]
    row_of = rows[...]
    owner = lax.div(row_of, own)
    local = (row_of - owner * own).astype(F32)
    lane = iota((1, count_rows), 1)
    half = count_rows // 2
    live = jnp.where(lane < half, lane, lane - half) < jnp.where(lane < half, counts[0], counts[1])
    hits = (iota((group, count_rows), 0) == owner).astype(F32)
    before = (iota((count_rows, count_rows), 0) < iota((count_rows, count_rows), 1)).astype(F32).astype(BF16)
    earlier = jnp.dot(hits.astype(BF16), before, preferred_element_type=F32)
    rank = jnp.sum(hits * earlier, axis=0, keepdims=True)
    slot = jnp.where(live, owner.astype(F32) * SLOTS + rank, -1.0)
    pick = iota((group * SLOTS, count_rows), 0).astype(F32) == slot
    place = jnp.sum(jnp.where(pick, local, 0.0), axis=1, keepdims=True)
    pick = pick.astype(F32).astype(BF16)
    by_columns = (((1,), (1,)), ((), ()))
    payload = 0.0
    for part in split(wide[...]):
        payload += lax.dot_general(pick, part, by_columns, preferred_element_type=F32)
    payload = jnp.where(iota(payload.shape, 1) == columns, place, payload)
    slots_out[...] = payload.reshape(slots_out.shape)

    same = (iota((own, own), 0) == iota((own, own), 1)).astype(F32).astype(BF16)
    high, low = split(rhs_wide[...])
    rest = (rhs_wide[...] - high.astype(F32) - low.astype(F32)).astype(BF16)
    rhs_rows = 0.0
    for part in (rest, low, high):
        rhs_rows += lax.dot_general(same, part, by_columns, preferred_element_type=F32)

    @pl.when(odd == 1)
    def _():
        order(sorted_first, 0)

    ends = (chain == 0) | last

    @pl.when(ends)
    def _():
        pl.semaphore_wait(barrier, group - 1 + SIDE)

    @pl.when(jnp.logical_not(ends))
    def _():
        pl.semaphore_wait(barrier, group - 1 + 2 * SIDE)

    def send_slots(offset, carry):
        peer = (me + offset) % group
        remote(slots_out.at[peer], slots_in.at[me], slot_send, slot_recv, (chain, peer)).start()
        return carry

    def columns_of(source, row):
        return source.at[:, :, pl.ds(pl.multiple_of(row * span, span), span)]

    def send_even(source, target, which):
        pltpu.make_async_copy(columns_of(source, along), target.at[along], local_sem.at[which]).start()
        for offset in (4, 3, 5, 2, 6, 1, 7):
            row = (along + offset) % SIDE
            remote(columns_of(source, row), target.at[along], mat_send.at[which], mat_recv.at[which],
                   (chain, place_of(across, row))).start()

    def send_odd(ordered, target, which):
        pltpu.make_async_copy(ordered.at[along], target.at[along], local_sem.at[which]).start()
        for offset in (4, 3, 5, 2, 6, 1, 7):
            row = (along + offset) % SIDE
            remote(ordered.at[row], target.at[along], mat_send.at[which], mat_recv.at[which],
                   (chain, place_of(across, row))).start()

    def take_matrix(target, which, hi, lo):
        pltpu.make_async_copy(target.at[along], target.at[along], local_sem.at[which]).wait()
        seven = target.at[pl.ds(0, SIDE - 1)]
        remote(seven, seven, mat_send.at[which], mat_recv.at[which], (chain, me)).wait_recv()

        def cut(row, carry):
            for part in range(2):
                high, low = split(target[row, part])
                at = pl.ds(pl.multiple_of(row * own, own), own)
                hi[at, part * span:(part + 1) * span] = high
                lo[at, part * span:(part + 1) * span] = low
            return carry

        lax.fori_loop(0, SIDE, cut, 0)

    slots_in[me] = slots_out[me]

    @pl.when(odd == 0)
    def _():
        lax.fori_loop(1, group, send_slots, 0)
        send_even(coup, first, 0)

    @pl.when(odd == 1)
    def _():
        send_odd(sorted_first, first, 0)
        take_matrix(first, 0, first_hi, first_lo)
        lax.fori_loop(1, group, send_slots, 0)

    most = slots_in.at[pl.ds(0, group - 1)]
    remote(most, most, slot_send, slot_recv, (chain, me)).wait_recv()
    arrived = slots_in[...].reshape(group * SLOTS, slots_in.shape[2])
    pick = (arrived[:, columns:columns + 1] == iota((group * SLOTS, own), 1).astype(F32)).astype(F32).astype(BF16)
    high, low = split(arrived)
    by_rows = (((0,), (0,)), ((), ()))
    total = (lax.dot_general(pick, high, by_rows, preferred_element_type=F32)
             + lax.dot_general(pick, low, by_rows, preferred_element_type=F32))
    total = rhs_rows - total
    for piece in range(pieces):
        column = piece * width
        tile = total[:, column // LANES * LANES:column // LANES * LANES + LANES]
        parts = []
        for index in range(fold):
            turn = (index * width - column) % LANES
            part = tile[index * fold_rows:(index + 1) * fold_rows]
            parts.append(pltpu.roll(part, turn, 1) if turn else part)
        base[piece] = folded(parts)

    @pl.when(odd == 0)
    def _():
        take_matrix(first, 0, first_hi, first_lo)

    def send_second():
        @pl.when(odd == 0)
        def _():
            send_even(diag, second, 1)

        @pl.when((odd == 1) & not_last)
        def _():
            load(diag, 1)
            order(sorted_second, 1)
            send_odd(sorted_second, second, 1)

    late = chain < chains // 2

    @pl.when(jnp.logical_not(late))
    def _():
        send_second()

    def begin(piece):
        @pl.when(chain == 0)
        def _():
            zbuf[piece, across] = base[piece]

        @pl.when(chain > 0)
        def _():
            remote(part_in.at[piece], part_in.at[piece], y_send.at[piece], y_recv.at[piece], (chain, me)).wait_recv()
            zbuf[piece, across] = base[piece] - jnp.sum(part_in[piece], axis=0)

        for offset in (4, 3, 5, 2, 6, 1, 7):
            peer = (across + offset) % SIDE
            remote(zbuf.at[piece, across], zbuf.at[piece, across], z_send.at[piece], z_recv.at[piece],
                   (chain, place_of(peer, along))).start()

    def multiply(piece, hi, lo, target):
        both = stack[piece]
        wide_sum = jnp.dot(hi[...], both, preferred_element_type=F32)
        narrow = jnp.dot(lo[...], both[:, :LANES], preferred_element_type=F32)
        sums = wide_sum[:, :LANES] + wide_sum[:, LANES:] + narrow
        for row in range(SIDE):
            target[piece, row] = folded(
                [sums[row * own + at * fold_rows:row * own + (at + 1) * fold_rows] for at in range(fold)])

    def send_diag(piece):
        diag_in[piece, along] = diag_out[piece, along]
        for offset in (4, 3, 5, 2, 6, 1, 7):
            row = (along + offset) % SIDE
            remote(diag_out.at[piece, row], diag_in.at[piece, along], d_send.at[piece], d_recv.at[piece],
                   (chain, place_of(across, row))).start()

    def finish(piece):
        seven = zbuf.at[piece, pl.ds(0, SIDE - 1)]
        remote(seven, seven, z_send.at[piece], z_recv.at[piece], (chain, me)).wait_recv()
        lane = iota((fold_rows, LANES), 1)
        imag = lane % width >= some
        for source in range(SIDE):
            block = zbuf[piece, source]
            turned = jnp.where(imag, pltpu.roll(block, some, 1), -pltpu.roll(block, LANES - some, 1))
            for part, value in enumerate((block, turned)):
                for index, wanted in enumerate(spread(value)):
                    high, low = split(wanted)
                    at = part * span + source * own + index * fold_rows
                    stack[piece, at:at + fold_rows, :LANES] = high
                    stack[piece, at:at + fold_rows, LANES:] = low

        @pl.when(not_last)
        def _():
            multiply(piece, first_hi, first_lo, part_out)
            for row in range(SIDE):
                remote(part_out.at[piece, row], part_in.at[piece, along], y_send.at[piece], y_recv.at[piece],
                       (chain + 1, place_of(across, row))).start()

        @pl.when(last)
        def _():
            multiply(piece, first_hi, first_lo, diag_out)
            send_diag(piece)

    def step(index, carry):
        @pl.when(index < pieces)
        def _():
            begin(index)

        @pl.when(index > 0)
        def _():
            finish(index - 1)

        return carry

    lax.fori_loop(0, pieces + 1, step, 0)

    @pl.when(late & (odd == 1))
    def _():
        pl.semaphore_signal(core_done, inc=1, device_id=(chain - 1, me), device_id_type=MESH)
        send_second()

    @pl.when(late & (odd == 0))
    def _():
        pl.semaphore_wait(core_done, 1)
        send_second()

    @pl.when(not_last)
    def _():
        take_matrix(second, 1, second_hi, second_lo)

        def solve(piece, carry):
            multiply(piece, second_hi, second_lo, diag_out)
            send_diag(piece)
            return carry

        lax.fori_loop(0, pieces, solve, 0)

    def collect(piece, carry):
        seven = diag_in.at[piece, pl.ds(0, SIDE - 1)]
        remote(seven, seven, d_send.at[piece], d_recv.at[piece], (chain, me)).wait_recv()
        out[piece] = jnp.sum(diag_in[piece], axis=0)
        return carry

    lax.fori_loop(0, pieces, collect, 0)

    remote(most, most, slot_send, slot_recv, (chain, me)).wait_send()
    seven = first.at[pl.ds(0, SIDE - 1)]
    remote(seven, seven, mat_send.at[0], mat_recv.at[0], (chain, me)).wait_send()

    @pl.when(not_last)
    def _():
        seven = second.at[pl.ds(0, SIDE - 1)]
        remote(seven, seven, mat_send.at[1], mat_recv.at[1], (chain, me)).wait_send()

    def drain(piece, carry):
        seven = zbuf.at[piece, pl.ds(0, SIDE - 1)]
        remote(seven, seven, z_send.at[piece], z_recv.at[piece], (chain, me)).wait_send()
        seven = diag_out.at[piece, pl.ds(0, SIDE - 1)]
        remote(seven, seven, d_send.at[piece], d_recv.at[piece], (chain, me)).wait_send()

        @pl.when(not_last)
        def _():
            remote(part_out.at[piece], part_out.at[piece], y_send.at[piece], y_recv.at[piece], (chain, me)).wait_send()

        return carry

    lax.fori_loop(0, pieces, drain, 0)


def body(chains, right_side, diag_inverse, coupling, updates, update_rows, tile_counts):
    batches, halves, sources, own = right_side.shape
    fold = FOLD
    fold_rows, width = own // fold, LANES // fold
    pieces = batches * halves * sources // width
    group = SIDE * SIDE
    span = SIDE * own
    count_rows = updates.shape[0]
    vmem = pl.BlockSpec(memory_space=pltpu.VMEM)
    hbm = pl.BlockSpec(memory_space=pltpu.HBM)
    block = (pieces, SIDE, fold_rows, LANES)
    dma = pltpu.SemaphoreType.DMA
    solved = pl.pallas_call(
        functools.partial(kernel, chains),
        out_shape=jax.ShapeDtypeStruct((pieces, fold_rows, LANES), F32),
        in_specs=[vmem, vmem, vmem, pl.BlockSpec(memory_space=pltpu.SMEM), hbm, hbm],
        out_specs=vmem,
        scratch_shapes=[
            pltpu.VMEM((2 * LANES, count_rows), F32),
            pltpu.VMEM((group, SLOTS, 2 * LANES), F32),
            pltpu.VMEM((group, SLOTS, 2 * LANES), F32),
            pltpu.VMEM((2, own, group * own), F32),
            pltpu.VMEM((SIDE, 2, own, span), F32),
            pltpu.VMEM((SIDE, 2, own, span), F32),
            pltpu.VMEM((SIDE, 2, own, span), F32),
            pltpu.VMEM((SIDE, 2, own, span), F32),
            pltpu.VMEM((span, 2 * span), BF16),
            pltpu.VMEM((span, 2 * span), BF16),
            pltpu.VMEM((span, 2 * span), BF16),
            pltpu.VMEM((span, 2 * span), BF16),
            pltpu.VMEM((2 * LANES, own), F32),
            pltpu.VMEM((pieces, fold_rows, LANES), F32),
            pltpu.VMEM(block, F32),
            pltpu.VMEM(block, F32),
            pltpu.VMEM(block, F32),
            pltpu.VMEM(block, F32),
            pltpu.VMEM(block, F32),
            pltpu.VMEM((pieces, 2 * span, 2 * LANES), BF16),
            dma((2,)),
            dma,
            dma,
            dma((2,)),
            dma((2,)),
            dma((pieces,)),
            dma((pieces,)),
            dma((pieces,)),
            dma((pieces,)),
            dma((pieces,)),
            dma((pieces,)),
            pltpu.SemaphoreType.REGULAR,
        ],
        compiler_params=pltpu.CompilerParams(collective_id=0, has_side_effects=True, vmem_limit_bytes=63 << 20),
    )(right_side.reshape(batches * halves * sources, own), updates.T, update_rows.reshape(1, count_rows), tile_counts, diag_inverse, coupling)
    solved = solved.reshape(batches, pieces // batches, fold_rows, fold, halves, width // halves)
    return solved.transpose(0, 4, 1, 5, 3, 2).reshape(right_side.shape)


def solution(mesh):
    in_specs = (
        P(None, None, None, ("chain", "tile")),
        P(None, ("chain", "tile"), None),
        P(None, ("chain", "tile"), None),
        P(("chain", "tile"), None),
        P(("chain", "tile")),
        P(("chain", "tile")),
    )
    out_specs = P(None, None, None, ("chain", "tile"))
    run = functools.partial(body, mesh.shape["chain"])
    return jax.shard_map(run, mesh=mesh, in_specs=in_specs, out_specs=out_specs, check_vma=False)
```

time: 217 us -> 150 us (0.69)
  Pallas kernels: 208 us -> 147 us
  local copies, waits for them, and re-layouts: 8.11 us -> 2.39 us
    pallas_call x1, Pallas kernels: 208 us -> 147 us  [body(): pl.pallas_call(functools.partial(kernel, chains), out_shape=jax.ShapeDtyp...]
    unnamed x9 -> x0, local copies, waits for them, and re-layouts: 5.57 us -> none
where the time goes in v2:
time: 150 us
  Pallas kernels  147 us (98%)
  local copies, waits for them, and re-layouts  2.39 us (2%)
    pallas_call x1, Pallas kernels, body(): pl.pallas_call(functools.partial(kernel, chains), out_shape=jax.ShapeDtyp...  147 us

profile of v2, /device:TPU:7, one launch (start us, length us, event | category | flops | bytes accessed | tf_op | source)
XLA Modules:
  0.0 149.5 jit_solution(10239877091180709322)
XLA Ops:
  0.0 147.1 %shard_map.64 = f32[6,16,128]{2,1,0:T(8,128)} custom-call(f32[192,64]{1,0:T(8,128)} %bitcast.6, f32[192,256]{1,0:T(8,128)} %bitcast.5, s32[1,256]{1,0:T(1,128)} %bitcast.7, s32[2]{0:T(128)} %counts.1, f32[2,64,4096]{2,1,0:T(8,128)} %diag.1, f32[2,64,4096]{2,1,0:T(8,128)} %coup.1), custom_call_target="tpu_custom_call" | custom-call | tf_op jit(solution)/shard_map/pallas_call | solution.py:396
  147.1 1.3 reshape.14
  148.5 0.2 copy.7
  148.7 0.8 reshape.15

commit v3 on v2

--- a/solution.py
+++ b/solution.py
@@ -194,28 +194,31 @@
         seven = target.at[pl.ds(0, SIDE - 1)]
         remote(seven, seven, mat_send.at[which], mat_recv.at[which], (chain, me)).wait_recv()
 
+        shift = (SIDE + 2 - across) % SIDE * own
+        half_span = span // 2
+
         def cut(row, carry):
             for part in range(2):
-                high, low = split(target[row, part])
+                high, low = split(pltpu.roll(target[row, part], shift, 1))
                 at = pl.ds(pl.multiple_of(row * own, own), own)
-                hi[at, part * span:(part + 1) * span] = high
-                lo[at, part * span:(part + 1) * span] = low
+                for side in range(2):
+                    here = side * span + part * half_span
+                    hi[at, here:here + half_span] = high[:, side * half_span:(side + 1) * half_span]
+                    lo[at, here:here + half_span] = low[:, side * half_span:(side + 1) * half_span]
             return carry
 
         lax.fori_loop(0, SIDE, cut, 0)
 
+    lax.fori_loop(1, group, send_slots, 0)
     slots_in[me] = slots_out[me]
 
     @pl.when(odd == 0)
     def _():
-        lax.fori_loop(1, group, send_slots, 0)
         send_even(coup, first, 0)
 
     @pl.when(odd == 1)
     def _():
         send_odd(sorted_first, first, 0)
-        take_matrix(first, 0, first_hi, first_lo)
-        lax.fori_loop(1, group, send_slots, 0)
 
     most = slots_in.at[pl.ds(0, group - 1)]
     remote(most, most, slot_send, slot_recv, (chain, me)).wait_recv()
@@ -236,10 +239,6 @@
             parts.append(pltpu.roll(part, turn, 1) if turn else part)
         base[piece] = folded(parts)
 
-    @pl.when(odd == 0)
-    def _():
-        take_matrix(first, 0, first_hi, first_lo)
-
     def send_second():
         @pl.when(odd == 0)
         def _():
@@ -251,12 +250,6 @@
             order(sorted_second, 1)
             send_odd(sorted_second, second, 1)
 
-    late = chain < chains // 2
-
-    @pl.when(jnp.logical_not(late))
-    def _():
-        send_second()
-
     def begin(piece):
         @pl.when(chain == 0)
         def _():
@@ -269,54 +262,76 @@
 
         for offset in (4, 3, 5, 2, 6, 1, 7):
             peer = (across + offset) % SIDE
-            remote(zbuf.at[piece, across], zbuf.at[piece, across], z_send.at[piece], z_recv.at[piece],
+            side = 0 if offset in (1, 2, 7) else 1
+            remote(zbuf.at[piece, across], zbuf.at[piece, across], z_send.at[piece], z_recv.at[piece, side],
                    (chain, place_of(peer, along))).start()
 
-    def multiply(piece, hi, lo, target):
-        both = stack[piece]
-        wide_sum = jnp.dot(hi[...], both, preferred_element_type=F32)
-        narrow = jnp.dot(lo[...], both[:, :LANES], preferred_element_type=F32)
-        sums = wide_sum[:, :LANES] + wide_sum[:, LANES:] + narrow
+    @pl.when(chain == 0)
+    def _():
+        def start(piece, carry):
+            begin(piece)
+            return carry
+
+        lax.fori_loop(0, pieces, start, 0)
+
+    take_matrix(first, 0, first_hi, first_lo)
+
+    late = chain < chains // 2
+
+    @pl.when(jnp.logical_not(late))
+    def _():
+        send_second()
+
+    def product(hi, lo, both):
+        wide_sum = jnp.dot(hi, both, preferred_element_type=F32)
+        narrow = jnp.dot(lo, both[:, :LANES], preferred_element_type=F32)
+        return wide_sum[:, :LANES] + wide_sum[:, LANES:] + narrow
+
+    def store(piece, sums, target):
         for row in range(SIDE):
             target[piece, row] = folded(
                 [sums[row * own + at * fold_rows:row * own + (at + 1) * fold_rows] for at in range(fold)])
 
-    def send_diag(piece):
-        diag_in[piece, along] = diag_out[piece, along]
+    def send_diag(piece, source):
+        diag_in[piece, along] = source[piece, along]
         for offset in (4, 3, 5, 2, 6, 1, 7):
             row = (along + offset) % SIDE
-            remote(diag_out.at[piece, row], diag_in.at[piece, along], d_send.at[piece], d_recv.at[piece],
+            remote(source.at[piece, row], diag_in.at[piece, along], d_send.at[piece], d_recv.at[piece],
                    (chain, place_of(across, row))).start()
 
     def finish(piece):
-        seven = zbuf.at[piece, pl.ds(0, SIDE - 1)]
-        remote(seven, seven, z_send.at[piece], z_recv.at[piece], (chain, me)).wait_recv()
         lane = iota((fold_rows, LANES), 1)
         imag = lane % width >= some
-        for source in range(SIDE):
-            block = zbuf[piece, source]
-            turned = jnp.where(imag, pltpu.roll(block, some, 1), -pltpu.roll(block, LANES - some, 1))
-            for part, value in enumerate((block, turned)):
-                for index, wanted in enumerate(spread(value)):
-                    high, low = split(wanted)
-                    at = part * span + source * own + index * fold_rows
-                    stack[piece, at:at + fold_rows, :LANES] = high
-                    stack[piece, at:at + fold_rows, LANES:] = low
+        sums = 0.0
+        for side in range(2):
+            some_blocks = zbuf.at[piece, pl.ds(0, 3 + side)]
+            remote(some_blocks, some_blocks, z_send.at[piece], z_recv.at[piece, side], (chain, me)).wait_recv()
+            for near in range(SIDE // 2):
+                block = zbuf[piece, (across + side * (SIDE // 2) + near + SIDE - 2) % SIDE]
+                turned = jnp.where(imag, pltpu.roll(block, some, 1), -pltpu.roll(block, LANES - some, 1))
+                for part, value in enumerate((block, turned)):
+                    for index, wanted in enumerate(spread(value)):
+                        high, low = split(wanted)
+                        at = side * span + part * (span // 2) + near * own + index * fold_rows
+                        stack[piece, at:at + fold_rows, :LANES] = high
+                        stack[piece, at:at + fold_rows, LANES:] = low
+            at = slice(side * span, (side + 1) * span)
+            sums = sums + product(first_hi[:, at], first_lo[:, at], stack[piece, at])
+        store(piece, sums, part_out)
 
         @pl.when(not_last)
         def _():
-            multiply(piece, first_hi, first_lo, part_out)
-            for row in range(SIDE):
+            for offset in (4, 3, 5, 2, 6, 1, 7, 0):
+                row = (along + offset) % SIDE
                 remote(part_out.at[piece, row], part_in.at[piece, along], y_send.at[piece], y_recv.at[piece],
                        (chain + 1, place_of(across, row))).start()
 
         @pl.when(last)
         def _():
-            multiply(piece, first_hi, first_lo, diag_out)
-            send_diag(piece)
+            send_diag(piece, part_out)
 
     def step(index, carry):
-        @pl.when(index < pieces)
+        @pl.when((index < pieces) & (chain > 0))
         def _():
             begin(index)
 
@@ -343,8 +358,8 @@
         take_matrix(second, 1, second_hi, second_lo)
 
         def solve(piece, carry):
-            multiply(piece, second_hi, second_lo, diag_out)
-            send_diag(piece)
+            store(piece, product(second_hi[...], second_lo[...], stack[piece]), diag_out)
+            send_diag(piece, diag_out)
             return carry
 
         lax.fori_loop(0, pieces, solve, 0)
@@ -368,7 +383,7 @@
 
     def drain(piece, carry):
         seven = zbuf.at[piece, pl.ds(0, SIDE - 1)]
-        remote(seven, seven, z_send.at[piece], z_recv.at[piece], (chain, me)).wait_send()
+        remote(seven, seven, z_send.at[piece], z_recv.at[piece, 0], (chain, me)).wait_send()
         seven = diag_out.at[piece, pl.ds(0, SIDE - 1)]
         remote(seven, seven, d_send.at[piece], d_recv.at[piece], (chain, me)).wait_send()
 
@@ -425,7 +440,7 @@
             dma((2,)),
             dma((2,)),
             dma((pieces,)),
-            dma((pieces,)),
+            dma((pieces, 2)),
             dma((pieces,)),
             dma((pieces,)),
             dma((pieces,)),

time: 150 us -> 142 us (0.947)
  Pallas kernels: 147 us -> 140 us
    pallas_call x1, Pallas kernels: 147 us -> 140 us  [body(): pl.pallas_call(functools.partial(kernel, chains), out_shape=jax.ShapeDtyp...]
where the time goes in v3:
time: 142 us
  Pallas kernels  140 us (99%)
  local copies, waits for them, and re-layouts  2.39 us (2%)
    pallas_call x1, Pallas kernels, body(): pl.pallas_call(functools.partial(kernel, chains), out_shape=jax.ShapeDtyp...  140 us

profile of v3, /device:TPU:7, one launch (start us, length us, event | category | flops | bytes accessed | tf_op | source)
XLA Modules:
  0.0 142.1 jit_solution(3507516804129374364)
XLA Ops:
  0.0 139.7 %shard_map.64 = f32[6,16,128]{2,1,0:T(8,128)} custom-call(f32[192,64]{1,0:T(8,128)} %bitcast.6, f32[192,256]{1,0:T(8,128)} %bitcast.5, s32[1,256]{1,0:T(1,128)} %bitcast.7, s32[2]{0:T(128)} %counts.1, f32[2,64,4096]{2,1,0:T(8,128)} %diag.1, f32[2,64,4096]{2,1,0:T(8,128)} %coup.1), custom_call_target="tpu_custom_call" | custom-call | tf_op jit(solution)/shard_map/pallas_call | solution.py:411
  139.7 1.3 reshape.14
  141.0 0.2 copy.7
  141.2 0.8 reshape.15

commit v4 on v3

--- a/solution.py
+++ b/solution.py
@@ -12,6 +12,7 @@
 BF16 = jnp.bfloat16
 SIDE = 8
 FOLD = 4
+AHEAD = 3
 SLOTS = 8
 LANES = 128
 
@@ -335,13 +336,13 @@
         def _():
             begin(index)
 
-        @pl.when(index > 0)
-        def _():
-            finish(index - 1)
+        @pl.when(index >= AHEAD)
+        def _():
+            finish(index - AHEAD)
 
         return carry
 
-    lax.fori_loop(0, pieces + 1, step, 0)
+    lax.fori_loop(0, pieces + AHEAD, step, 0)
 
     @pl.when(late & (odd == 1))
     def _():

time: 142 us -> 137 us (0.965)
  Pallas kernels: 140 us -> 135 us
    pallas_call x1, Pallas kernels: 140 us -> 135 us  [body(): pl.pallas_call(functools.partial(kernel, chains), out_shape=jax.ShapeDtyp...]
where the time goes in v4:
time: 137 us
  Pallas kernels  135 us (99%)
  local copies, waits for them, and re-layouts  2.39 us (2%)
    pallas_call x1, Pallas kernels, body(): pl.pallas_call(functools.partial(kernel, chains), out_shape=jax.ShapeDtyp...  135 us

profile of v4, /device:TPU:7, one launch (start us, length us, event | category | flops | bytes accessed | tf_op | source)
XLA Modules:
  0.0 137.1 jit_solution(12101511099305172011)
XLA Ops:
  0.0 134.6 %shard_map.64 = f32[6,16,128]{2,1,0:T(8,128)} custom-call(f32[192,64]{1,0:T(8,128)} %bitcast.6, f32[192,256]{1,0:T(8,128)} %bitcast.5, s32[1,256]{1,0:T(1,128)} %bitcast.7, s32[2]{0:T(128)} %counts.1, f32[2,64,4096]{2,1,0:T(8,128)} %diag.1, f32[2,64,4096]{2,1,0:T(8,128)} %coup.1), custom_call_target="tpu_custom_call" | custom-call | tf_op jit(solution)/shard_map/pallas_call | solution.py:412
  134.7 1.3 reshape.14
  136.0 0.2 copy.7
  136.2 0.8 reshape.15

commit v5 on v4

--- a/solution.py
+++ b/solution.py
@@ -210,16 +210,17 @@
 
         lax.fori_loop(0, SIDE, cut, 0)
 
-    lax.fori_loop(1, group, send_slots, 0)
     slots_in[me] = slots_out[me]
 
     @pl.when(odd == 0)
     def _():
+        lax.fori_loop(1, group, send_slots, 0)
         send_even(coup, first, 0)
 
     @pl.when(odd == 1)
     def _():
         send_odd(sorted_first, first, 0)
+        lax.fori_loop(1, group, send_slots, 0)
 
     most = slots_in.at[pl.ds(0, group - 1)]
     remote(most, most, slot_send, slot_recv, (chain, me)).wait_recv()

time: 137 us -> 138 us (level)
  no operation moved by 1% of the time
where the time goes in v5:
time: 138 us; the launch traced here: 137 us
  Pallas kernels  135 us (98%)
  local copies, waits for them, and re-layouts  2.39 us (2%)
    pallas_call x1, Pallas kernels, body(): pl.pallas_call(functools.partial(kernel, chains), out_shape=jax.ShapeDtyp...  135 us

profile of v5, /device:TPU:7, one launch (start us, length us, event | category | flops | bytes accessed | tf_op | source)
XLA Modules:
  0.0 137.5 jit_solution(4635692126032542711)
XLA Ops:
  0.0 135.1 %shard_map.64 = f32[6,16,128]{2,1,0:T(8,128)} custom-call(f32[192,64]{1,0:T(8,128)} %bitcast.6, f32[192,256]{1,0:T(8,128)} %bitcast.5, s32[1,256]{1,0:T(1,128)} %bitcast.7, s32[2]{0:T(128)} %counts.1, f32[2,64,4096]{2,1,0:T(8,128)} %diag.1, f32[2,64,4096]{2,1,0:T(8,128)} %coup.1), custom_call_target="tpu_custom_call" | custom-call | tf_op jit(solution)/shard_map/pallas_call | solution.py:413
  135.1 1.3 reshape.14
  136.4 0.2 copy.7
  136.6 0.8 reshape.15
